TPU v7x, 512 devices: a whole 4x4x16 slice. The times are simulated.
512 devices in a mesh: pipe: 8 (over x, core), dp: 64 (over y, z).
Axes of the slice: x: 4, y: 4, z: 16, core: 2. Of those that a mesh axis runs over, the one named last changes fastest.
Arguments:
- saved_inputs: bfloat16 [8, 8192, 8192], P('pipe', 'dp'), may hold values from -1000 to 1000
- cotangent: bfloat16 [8192, 8192], P('dp', 'pipe'), may hold values from -500 to 500
- weights_bf16: bfloat16 [8, 2, 64, 8192], P('pipe', None, None, 'dp'), may hold values from -6 to 6
- master: float32 [8, 2, 64, 8192], P('pipe', None, None, 'dp'), may hold values from -6 to 6
- moment1: float32 [8, 2, 64, 8192], P('pipe', None, None, 'dp'), may hold values from -6 to 6
- moment2: float32 [8, 2, 64, 8192], P('pipe', None, None, 'dp'), may hold values from 0.5 to 8
- valid_rows: int32 [64], P('dp'), may hold values from 1 to 128, 6144 in all
Outputs:
- new_master: float32 [8, 2, 64, 8192], P('pipe', None, None, 'dp')
- new_moment1: float32 [8, 2, 64, 8192], P('pipe', None, None, 'dp')
- new_moment2: float32 [8, 2, 64, 8192], P('pipe', None, None, 'dp')
- new_weights: bfloat16 [8, 2, 64, 8192], P('pipe', None, None, 'dp')
Inputs may be any that keep to these rules, and one draw needn't show every extreme that they name: `valid_rows`: the counts sum to 6144.
All inputs are finite; a program needn't handle non-finite values. No bound on the sum of `valid_rows` on one device may be relied on, other than what follows from the above.
Results may differ from a plain program's by a relative error of at most 0.02.
Values may be sent and summed in bfloat16 or wider, within the bound.
No kernel may reach another device: no remote copies, remote signals or barrier semaphores. Data moves between devices by JAX's collectives and lax.ppermute only.
A program may use at most 64 MiB of HBM per device.

v0:
```python
import math
import jax
import jax.numpy as jnp
from jax import lax
from jax.sharding import PartitionSpec as P

BETA_ONE = 0.9
BETA_TWO = 0.95
LEARN_RATE = 0.05
DECAY_RATE = 0.1
ADAM_EPS = 1e-08
CLIP_RMS = 2.0
NORM_EPS = 1e-12


def shifted(x, axis, by):
    length = lax.axis_size(axis)
    pairs = [(i, i + by) for i in range(length) if 0 <= i + by < length]
    return lax.ppermute(x, axis, pairs)


def section_backward(inputs_block, incoming, weights):
    down_proj = weights[0]
    up_proj = weights[1]
    model_width = inputs_block.shape[1]
    adapter_rank = weights.shape[1]
    pre_act = lax.dot_general(
        inputs_block, down_proj, (((1,), (1,)), ((), ())), preferred_element_type=jnp.float32
    ) * (1.0 / math.sqrt(model_width))
    activated = jax.nn.silu(pre_act).astype(jnp.bfloat16)
    logistic = jax.nn.sigmoid(pre_act)
    derivative = logistic * (1.0 + pre_act * (1.0 - logistic))
    along_rank = lax.dot_general(
        incoming, up_proj, (((1,), (1,)), ((), ())), preferred_element_type=jnp.float32
    ) * (1.0 / math.sqrt(adapter_rank))
    back_grad = (along_rank * derivative).astype(jnp.bfloat16)
    grad_up = lax.dot_general(
        activated, incoming, (((0,), (0,)), ((), ())), preferred_element_type=jnp.float32
    ) * (1.0 / math.sqrt(adapter_rank))
    grad_down = lax.dot_general(
        back_grad, inputs_block, (((0,), (0,)), ((), ())), preferred_element_type=jnp.float32
    ) * (1.0 / math.sqrt(model_width))
    outgoing = (
        incoming.astype(jnp.float32)
        + jnp.dot(back_grad, down_proj, preferred_element_type=jnp.float32)
        * (1.0 / math.sqrt(model_width))
    ).astype(jnp.bfloat16)
    return (outgoing, jnp.stack([grad_down, grad_up]))


def body(saved_inputs, cotangent, weights_bf16, master, moment1, moment2, valid_rows):
    sections = lax.axis_size("pipe")
    section_index = lax.axis_index("pipe")
    weights = lax.all_gather(weights_bf16[0], "dp", axis=2, tiled=True)
    loss_grad = lax.all_gather(cotangent, "pipe", axis=1, tiled=True)
    inputs = saved_inputs[0]
    row_count = inputs.shape[0]
    model_width = inputs.shape[1]
    adapter_rank = weights.shape[1]
    live_rows = jnp.arange(row_count, dtype=jnp.int32) < valid_rows[0]
    loss_grad = jnp.where(live_rows[:, None], loss_grad, jnp.zeros_like(loss_grad))
    blocks = 1
    block_rows = row_count // blocks
    grad_shape = (2, adapter_rank, model_width)

    def chain_turn(step_index, state_pair):
        gradients, received = state_pair
        position = step_index - (sections - 1 - section_index)
        active = (position >= 0) & (position < blocks)
        incoming = jnp.where(section_index == sections - 1, loss_grad, received)

        def compute():
            return section_backward(inputs, incoming, weights)

        def skipped():
            return (
                jnp.zeros((block_rows, model_width), jnp.bfloat16),
                jnp.zeros(grad_shape, jnp.float32),
            )

        outgoing, grad_part = lax.cond(active, compute, skipped)
        received = shifted(outgoing, "pipe", -1)
        return (gradients + grad_part, received)

    start_pair = (
        jnp.zeros(grad_shape, jnp.float32),
        jnp.zeros((block_rows, model_width), jnp.bfloat16),
    )
    gradients, unused = lax.fori_loop(0, sections + blocks - 1, chain_turn, start_pair)
    grad_shard = lax.psum_scatter(gradients, "dp", scatter_dimension=2, tiled=True)
    square_sum = lax.psum(jnp.sum(grad_shard * grad_shard), ("pipe", "dp"))
    norm_limit = CLIP_RMS * math.sqrt(2.0 * sections * adapter_rank * model_width)
    clip_factor = jnp.minimum(1.0, norm_limit / jnp.sqrt(square_sum + NORM_EPS))
    scaled = grad_shard * clip_factor
    new_moment1 = BETA_ONE * moment1[0] + (1.0 - BETA_ONE) * scaled
    new_moment2 = BETA_TWO * moment2[0] + (1.0 - BETA_TWO) * scaled * scaled
    new_master = master[0] - LEARN_RATE * (
        new_moment1 / (jnp.sqrt(new_moment2) + ADAM_EPS) + DECAY_RATE * master[0]
    )
    return (
        new_master[None],
        new_moment1[None],
        new_moment2[None],
        new_master.astype(jnp.bfloat16)[None],
    )


def solution(mesh):
    in_specs = (
        P("pipe", "dp", None),
        P("dp", "pipe"),
        P("pipe", None, None, "dp"),
        P("pipe", None, None, "dp"),
        P("pipe", None, None, "dp"),
        P("pipe", None, None, "dp"),
        P("dp"),
    )
    out_specs = (
        P("pipe", None, None, "dp"),
        P("pipe", None, None, "dp"),
        P("pipe", None, None, "dp"),
        P("pipe", None, None, "dp"),
    )
    return jax.shard_map(body, mesh=mesh, in_specs=in_specs, out_specs=out_specs, check_vma=False)
```

profile of v0, /device:TPU:1, one launch (start us, length us, event | category | flops | bytes accessed | tf_op | source)
XLA Modules:
  0.0 1259.6 jit_solution(12248657878223781486)
XLA Ops:
  9.4 39.3 %all-gather.4.cloned.1.call-done = bf16[128,8192]{1,0:T(8,128)(2,1)} async-done(((bf16[128,1024]{1,0:T(8,128)(2,1)}), bf16[128,8192]{1,0:T(8,128)(2,1)}) %all-gather.4.cloned.1.call-update) | async-done | bytes 2097168 | tf_op jit(solution)/shard_map/all_gather | solution.py:55
  48.7 3.1 broadcast_select_fusion.1
  51.8 126.0 %all-gather.6.cloned.1.call-done = bf16[1,2,64,8192]{3,2,1,0:T(8,128)(2,1)} async-done(((bf16[1,2,64,128]{3,2,1,0:T(8,128)(2,1)}), bf16[1,2,64,8192]{3,2,1,0:T(8,128)(2,1)}) %all-gather.6.cloned.1.call-update) | async-done | bytes 2097168 | tf_op jit(solution)/shard_map/all_gather | solution.py:54
  179.3 272.9 %while.18 = (s32[]{:T(128)}, f32[2,64,8192]{2,1,0:T(8,128)}, bf16[128,8192]{1,0:T(8,128)(2,1)}, s32[]{:T(128)}, pred[]{:T(512)}, /*index=5*/bf16[128,8192]{1,0:T...) while((s32[]{:T(128)}, f32[2,64,8192]{2,1,0:T(8,128)}, ...), condition=%wide.region_3.4_spmd.clone, body=%wide.region_0.3_spmd.clone.sunk | while | flops 680656896 | bytes 72499496 | solution.py:89
  179.3 3.9 conditional.3
  183.3 11.6 collective-permute-start
  194.9 4.7 select_add_fusion.2
  199.5 20.4 %collective-permute-done = bf16[128,8192]{1,0:T(8,128)(2,1)} collective-permute-done((bf16[128,8192]{1,0:T(8,128)(2,1)}, bf16[128,8192]{1,0:T(8,128)(2,1)}, u32[]{:S(2)}, u32[]{:S(2)}) %collective-permute-start) | collective-permute-done | bytes 2097184 | tf_op jit(solution)/shard_map/while/body/eval_jaxpr/ppermute | solution.py:19
  220.0 3.9 conditional.3
  220.0 2.4 broadcast.35
  225.8 5.9 select_add_fusion.2
  231.7 19.8 %collective-permute-done = bf16[128,8192]{1,0:T(8,128)(2,1)} collective-permute-done((bf16[128,8192]{1,0:T(8,128)(2,1)}, bf16[128,8192]{1,0:T(8,128)(2,1)}, u32[]{:S(2)}, u32[]{:S(2)}) %collective-permute-start) | collective-permute-done | bytes 2097184 | tf_op jit(solution)/shard_map/while/body/eval_jaxpr/ppermute | solution.py:19
  251.5 3.9 conditional.3
  257.3 5.9 select_add_fusion.2
  263.3 19.8 %collective-permute-done = bf16[128,8192]{1,0:T(8,128)(2,1)} collective-permute-done((bf16[128,8192]{1,0:T(8,128)(2,1)}, bf16[128,8192]{1,0:T(8,128)(2,1)}, u32[]{:S(2)}, u32[]{:S(2)}) %collective-permute-start) | collective-permute-done | bytes 2097184 | tf_op jit(solution)/shard_map/while/body/eval_jaxpr/ppermute | solution.py:19
  283.1 3.9 conditional.3
  288.9 5.9 select_add_fusion.2
  294.9 19.8 %collective-permute-done = bf16[128,8192]{1,0:T(8,128)(2,1)} collective-permute-done((bf16[128,8192]{1,0:T(8,128)(2,1)}, bf16[128,8192]{1,0:T(8,128)(2,1)}, u32[]{:S(2)}, u32[]{:S(2)}) %collective-permute-start) | collective-permute-done | bytes 2097184 | tf_op jit(solution)/shard_map/while/body/eval_jaxpr/ppermute | solution.py:19
  314.7 3.9 conditional.3
  320.5 5.9 select_add_fusion.2
  326.4 19.8 %collective-permute-done = bf16[128,8192]{1,0:T(8,128)(2,1)} collective-permute-done((bf16[128,8192]{1,0:T(8,128)(2,1)}, bf16[128,8192]{1,0:T(8,128)(2,1)}, u32[]{:S(2)}, u32[]{:S(2)}) %collective-permute-start) | collective-permute-done | bytes 2097184 | tf_op jit(solution)/shard_map/while/body/eval_jaxpr/ppermute | solution.py:19
  346.2 3.9 conditional.3
  352.1 5.9 select_add_fusion.2
  358.0 24.5 %collective-permute-done = bf16[128,8192]{1,0:T(8,128)(2,1)} collective-permute-done((bf16[128,8192]{1,0:T(8,128)(2,1)}, bf16[128,8192]{1,0:T(8,128)(2,1)}, u32[]{:S(2)}, u32[]{:S(2)}) %collective-permute-start) | collective-permute-done | bytes 2097184 | tf_op jit(solution)/shard_map/while/body/eval_jaxpr/ppermute | solution.py:19
  382.5 10.5 conditional.3
  395.0 5.9 select_add_fusion.2
  400.9 19.8 %collective-permute-done = bf16[128,8192]{1,0:T(8,128)(2,1)} collective-permute-done((bf16[128,8192]{1,0:T(8,128)(2,1)}, bf16[128,8192]{1,0:T(8,128)(2,1)}, u32[]{:S(2)}, u32[]{:S(2)}) %collective-permute-start) | collective-permute-done | bytes 2097184 | tf_op jit(solution)/shard_map/while/body/eval_jaxpr/ppermute | solution.py:19
  420.7 3.9 conditional.3
  426.5 5.9 select_add_fusion.2
  432.5 19.8 %collective-permute-done = bf16[128,8192]{1,0:T(8,128)(2,1)} collective-permute-done((bf16[128,8192]{1,0:T(8,128)(2,1)}, bf16[128,8192]{1,0:T(8,128)(2,1)}, u32[]{:S(2)}, u32[]{:S(2)}) %collective-permute-start) | collective-permute-done | bytes 2097184 | tf_op jit(solution)/shard_map/while/body/eval_jaxpr/ppermute | solution.py:19
  452.3 684.5 %reduce-scatter.2.cloned.1.call-done = f32[2,64,128]{2,1,0:T(8,128)} async-done(((f32[2,64,8192]{2,1,0:T(8,128)}), f32[2,64,128]{2,1,0:T(8,128)}) %reduce-scatter.2.cloned.1.call-update) | async-done | bytes 65552 | tf_op jit(solution)/shard_map/reduce_scatter | solution.py:90
  1138.2 112.5 %psum.7 = f32[]{:T(128)} all-reduce(f32[]{:T(128)} %multiply_reduce_fusion), channel_id=1, replica_groups=mesh['pipe'=8,'dp'=64] {'pipe','dp'}, use_global_device_ids=true, to_apply=%region_6.7 | all-reduce | flops 1 | bytes 8 | tf_op jit(solution)/shard_map/psum | solution.py:91
  (50 shorter events, 54.9 us)
Async XLA Ops:
  7.2 41.5 %all-gather.4.cloned.1.call-start = ((), (), s32[]{:S(2)}) async-start(), calls=%async_computation.1 | async-start | bytes 2359296 | tf_op jit(solution)/shard_map/all_gather | solution.py:55
  7.9 169.9 %all-gather.6.cloned.1.call-start = ((), (), s32[]{:S(2)}) async-start(), calls=%async_computation.3 | async-start | bytes 2129920 | tf_op jit(solution)/shard_map/all_gather | solution.py:54
  8.6 1128.1 %reduce-scatter.2.cloned.1.call-start = ((), (), s32[]{:S(2)}) async-start(), calls=%async_computation.2 | async-start | bytes 4259840 | tf_op jit(solution)/shard_map/reduce_scatter | solution.py:90
  51.8 127.5 %copy-start = (bf16[1,128,8192]{2,1,0:T(8,128)(2,1)S(1)}, bf16[1,128,8192]{2,1,0:T(8,128)(2,1)}, u32[]{:S(2)}) copy-start(bf16[1,128,8192]{2,1,0:T(8,128)(2,1)} %param.11) | copy-start | bytes 6291460
  183.3 36.7 %collective-permute-start = (bf16[128,8192]{1,0:T(8,128)(2,1)}, bf16[128,8192]{1,0:T(8,128)(2,1)}, u32[]{:S(2)}, u32[]{:S(2)}) collective-permute-start(bf16[128,8192]{1,0:T(8,128)(2,1)} %get-tuple-element.300), channel_id=1, source_target_pairs={{64,0},{128,64},{192,128},{256,192},{320,256},{384,320},{448,384},... | collective-permute-start | bytes 6291464 | tf_op jit(solution)/shard_map/while/body/eval_jaxpr/ppermute | solution.py:19
  223.9 27.7 %collective-permute-start = (bf16[128,8192]{1,0:T(8,128)(2,1)}, bf16[128,8192]{1,0:T(8,128)(2,1)}, u32[]{:S(2)}, u32[]{:S(2)}) collective-permute-start(bf16[128,8192]{1,0:T(8,128)(2,1)} %get-tuple-element.300), channel_id=1, source_target_pairs={{64,0},{128,64},{192,128},{256,192},{320,256},{384,320},{448,384},... | collective-permute-start | bytes 6291464 | tf_op jit(solution)/shard_map/while/body/eval_jaxpr/ppermute | solution.py:19
  255.4 27.7 %collective-permute-start = (bf16[128,8192]{1,0:T(8,128)(2,1)}, bf16[128,8192]{1,0:T(8,128)(2,1)}, u32[]{:S(2)}, u32[]{:S(2)}) collective-permute-start(bf16[128,8192]{1,0:T(8,128)(2,1)} %get-tuple-element.300), channel_id=1, source_target_pairs={{64,0},{128,64},{192,128},{256,192},{320,256},{384,320},{448,384},... | collective-permute-start | bytes 6291464 | tf_op jit(solution)/shard_map/while/body/eval_jaxpr/ppermute | solution.py:19
  287.0 27.7 %collective-permute-start = (bf16[128,8192]{1,0:T(8,128)(2,1)}, bf16[128,8192]{1,0:T(8,128)(2,1)}, u32[]{:S(2)}, u32[]{:S(2)}) collective-permute-start(bf16[128,8192]{1,0:T(8,128)(2,1)} %get-tuple-element.300), channel_id=1, source_target_pairs={{64,0},{128,64},{192,128},{256,192},{320,256},{384,320},{448,384},... | collective-permute-start | bytes 6291464 | tf_op jit(solution)/shard_map/while/body/eval_jaxpr/ppermute | solution.py:19
  318.6 27.7 %collective-permute-start = (bf16[128,8192]{1,0:T(8,128)(2,1)}, bf16[128,8192]{1,0:T(8,128)(2,1)}, u32[]{:S(2)}, u32[]{:S(2)}) collective-permute-start(bf16[128,8192]{1,0:T(8,128)(2,1)} %get-tuple-element.300), channel_id=1, source_target_pairs={{64,0},{128,64},{192,128},{256,192},{320,256},{384,320},{448,384},... | collective-permute-start | bytes 6291464 | tf_op jit(solution)/shard_map/while/body/eval_jaxpr/ppermute | solution.py:19
  350.1 32.4 %collective-permute-start = (bf16[128,8192]{1,0:T(8,128)(2,1)}, bf16[128,8192]{1,0:T(8,128)(2,1)}, u32[]{:S(2)}, u32[]{:S(2)}) collective-permute-start(bf16[128,8192]{1,0:T(8,128)(2,1)} %get-tuple-element.300), channel_id=1, source_target_pairs={{64,0},{128,64},{192,128},{256,192},{320,256},{384,320},{448,384},... | collective-permute-start | bytes 6291464 | tf_op jit(solution)/shard_map/while/body/eval_jaxpr/ppermute | solution.py:19
  382.5 2.2 copy-start.2
  384.7 2.2 copy-start.1
  393.0 27.7 %collective-permute-start = (bf16[128,8192]{1,0:T(8,128)(2,1)}, bf16[128,8192]{1,0:T(8,128)(2,1)}, u32[]{:S(2)}, u32[]{:S(2)}) collective-permute-start(bf16[128,8192]{1,0:T(8,128)(2,1)} %get-tuple-element.300), channel_id=1, source_target_pairs={{64,0},{128,64},{192,128},{256,192},{320,256},{384,320},{448,384},... | collective-permute-start | bytes 6291464 | tf_op jit(solution)/shard_map/while/body/eval_jaxpr/ppermute | solution.py:19
  424.6 27.7 %collective-permute-start = (bf16[128,8192]{1,0:T(8,128)(2,1)}, bf16[128,8192]{1,0:T(8,128)(2,1)}, u32[]{:S(2)}, u32[]{:S(2)}) collective-permute-start(bf16[128,8192]{1,0:T(8,128)(2,1)} %get-tuple-element.300), channel_id=1, source_target_pairs={{64,0},{128,64},{192,128},{256,192},{320,256},{384,320},{448,384},... | collective-permute-start | bytes 6291464 | tf_op jit(solution)/shard_map/while/body/eval_jaxpr/ppermute | solution.py:19
  452.3 799.2 %copy-start.3 = (f32[1,2,64,128]{3,2,1,0:T(8,128)S(1)}, f32[1,2,64,128]{3,2,1,0:T(8,128)}, u32[]{:S(2)}) copy-start(f32[1,2,64,128]{3,2,1,0:T(8,128)} %param.16) | copy-start | bytes 196612
  452.3 799.2 %copy-start.4 = (f32[1,2,64,128]{3,2,1,0:T(8,128)S(1)}, f32[1,2,64,128]{3,2,1,0:T(8,128)}, u32[]{:S(2)}) copy-start(f32[1,2,64,128]{3,2,1,0:T(8,128)} %param.15) | copy-start | bytes 196612
  452.3 799.2 %copy-start.5 = (f32[1,2,64,128]{3,2,1,0:T(8,128)S(1)}, f32[1,2,64,128]{3,2,1,0:T(8,128)}, u32[]{:S(2)}) copy-start(f32[1,2,64,128]{3,2,1,0:T(8,128)} %param.14) | copy-start | bytes 196612
Sparse Core Ops, SparseCore 0:
  10.1 38.5 all-gather.3
  51.6 126.1 all-gather.5
  452.4 684.2 reduce-scatter.1
where the time goes:
time: 1260 us
  waiting for transfers between devices  1010 us (80%)
  blocking collectives  113 us (9%)
  other arithmetic  56.6 us (4%)
  local copies, waits for them, and re-layouts  29.1 us (2%)
  starting transfers between devices  25.1 us (2%)
  between operations  15.1 us (1%)
    reduce_scatter x1, waiting for transfers between devices, body(): lax.psum_scatter(gradients, 'dp', scatter_dimension=2, tiled=True)  684 us
    ppermute x8, waiting for transfers between devices, shifted(): return lax.ppermute(x, axis, pairs)  164 us
    all_gather x1, waiting for transfers between devices, body(): weights = lax.all_gather(weights_bf16[0], 'dp', axis=2, tiled=True)  126 us
    psum x1, blocking collectives, body(): square_sum = lax.psum(jnp.sum(grad_shard * grad_shard), ('pipe', 'dp'))  113 us
    add x8, other arithmetic, chain_turn(): return (gradients + grad_part, received)  46.2 us
    all_gather x1, waiting for transfers between devices, body(): loss_grad = lax.all_gather(cotangent, 'pipe', axis=1, tiled=True)  39.3 us
    another operation x15, local copies, waits for them, and re-layouts  28.9 us
  transfers between devices with their start and end apart: 11, of which 11 were waited for; matrix products, arithmetic and copies ran while one was open for 4% of the time, Pallas kernels for 0%

commit v1 on v0

--- a/solution.py
+++ b/solution.py
@@ -51,7 +51,9 @@
 def body(saved_inputs, cotangent, weights_bf16, master, moment1, moment2, valid_rows):
     sections = lax.axis_size("pipe")
     section_index = lax.axis_index("pipe")
-    weights = lax.all_gather(weights_bf16[0], "dp", axis=2, tiled=True)
+    weights = jnp.concatenate(
+        lax.all_to_all(jnp.stack([weights_bf16[0]] * lax.axis_size("dp")), "dp", 0, 0), axis=2
+    )
     loss_grad = lax.all_gather(cotangent, "pipe", axis=1, tiled=True)
     inputs = saved_inputs[0]
     row_count = inputs.shape[0]

time: 1260 us -> 1200 us (0.952)
  waiting for transfers between devices: 1010 us -> 938 us
  starting transfers between devices: 25.1 us -> 38 us
    all_gather x1 -> x0, waiting for transfers between devices: 126 us -> none  [body(): weights = lax.all_gather(weights_bf16[0], 'dp', axis=2, tiled=True)]
    all_to_all x0 -> x1, waiting for transfers between devices: none -> 54.3 us  [body(): lax.all_to_all(jnp.stack([weights_bf16[0]] * lax.axis_size('dp')), 'dp',...]
    all_to_all x0 -> x1, starting transfers between devices: none -> 19.3 us  [body(): lax.all_to_all(jnp.stack([weights_bf16[0]] * lax.axis_size('dp')), 'dp',...]
    another operation x15 -> x16, local copies, waits for them, and re-layouts: 28.9 us -> 31.6 us
where the time goes in v1:
time: 1200 us
  waiting for transfers between devices  938 us (78%)
  blocking collectives  113 us (9%)
  other arithmetic  56.6 us (5%)
  starting transfers between devices  38 us (3%)
  local copies, waits for them, and re-layouts  34.3 us (3%)
  between operations  15.4 us (1%)
    reduce_scatter x1, waiting for transfers between devices, body(): lax.psum_scatter(gradients, 'dp', scatter_dimension=2, tiled=True)  683 us
    ppermute x8, waiting for transfers between devices, shifted(): return lax.ppermute(x, axis, pairs)  164 us
    psum x1, blocking collectives, body(): square_sum = lax.psum(jnp.sum(grad_shard * grad_shard), ('pipe', 'dp'))  113 us
    all_to_all x1, waiting for transfers between devices, body(): lax.all_to_all(jnp.stack([weights_bf16[0]] * lax.axis_size('dp')), 'dp',...  54.3 us
    add x8, other arithmetic, chain_turn(): return (gradients + grad_part, received)  46.2 us
    all_gather x1, waiting for transfers between devices, body(): loss_grad = lax.all_gather(cotangent, 'pipe', axis=1, tiled=True)  35.9 us
    another operation x15, local copies, waits for them, and re-layouts  28.9 us
  transfers between devices with their start and end apart: 11, of which 11 were waited for; matrix products, arithmetic and copies ran while one was open for 4% of the time, Pallas kernels for 0%

profile of v1, /device:TPU:1, one launch (start us, length us, event | category | flops | bytes accessed | tf_op | source)
XLA Modules:
  0.0 1200.7 jit_solution(9662742206500496153)
XLA Ops:
  9.8 19.3 %all-to-all-start = ((bf16[64,2,64,128]{3,2,1,0:T(8,128)(2,1)}), bf16[64,2,64,128]{3,2,1,0:T(8,128)(2,1)S(1)}, u32[]{:S(2)}, u32[]{:S(2)}) async-start(bf16[64,2,64,128]{3,2,1,0:T(8,128)(2,1)} %stack.12), calls=%async_computation | async-start | bytes 4194304 | tf_op jit(solution)/shard_map/all_to_all | solution.py:55
  30.5 35.9 %all-gather.2.cloned.1.call-done = bf16[128,8192]{1,0:T(8,128)(2,1)} async-done(((bf16[128,1024]{1,0:T(8,128)(2,1)}), bf16[128,8192]{1,0:T(8,128)(2,1)}) %all-gather.2.cloned.1.call-update) | async-done | bytes 2097168 | tf_op jit(solution)/shard_map/all_gather | solution.py:57
  66.5 3.2 broadcast_select_fusion.1
  69.6 54.3 %all-to-all-done = bf16[64,2,64,128]{3,2,1,0:T(8,128)(2,1)S(1)} async-done(((bf16[64,2,64,128]{3,2,1,0:T(8,128)(2,1)}), bf16[64,2,64,128]{3,2,1,0:T(8,128)(2,1)S(1)}, u32[]{:S(2)}, u32[]{:S(2)}) %all-to-all-start) | async-done | bytes 2097184 | tf_op jit(solution)/shard_map/all_to_all | solution.py:55
  127.9 266.7 %while.18 = (s32[]{:T(128)}, f32[2,64,8192]{2,1,0:T(8,128)}, bf16[128,8192]{1,0:T(8,128)(2,1)}, s32[]{:T(128)}, pred[]{:T(512)}, /*index=5*/bf16[128,8192]{1,0:T...) while((s32[]{:T(128)}, f32[2,64,8192]{2,1,0:T(8,128)}, ...), condition=%wide.region_3.4_spmd.clone, body=%wide.region_0.3_spmd.clone.sunk | while | flops 680656896 | bytes 72499496 | solution.py:91
  127.9 3.9 conditional.3
  131.8 5.3 collective-permute-start
  137.1 4.7 select_add_fusion.2
  141.8 20.5 %collective-permute-done = bf16[128,8192]{1,0:T(8,128)(2,1)} collective-permute-done((bf16[128,8192]{1,0:T(8,128)(2,1)}, bf16[128,8192]{1,0:T(8,128)(2,1)}, u32[]{:S(2)}, u32[]{:S(2)}) %collective-permute-start) | collective-permute-done | bytes 2097184 | tf_op jit(solution)/shard_map/while/body/eval_jaxpr/ppermute | solution.py:19
  162.2 3.9 conditional.3
  168.1 5.9 select_add_fusion.2
  174.0 19.8 %collective-permute-done = bf16[128,8192]{1,0:T(8,128)(2,1)} collective-permute-done((bf16[128,8192]{1,0:T(8,128)(2,1)}, bf16[128,8192]{1,0:T(8,128)(2,1)}, u32[]{:S(2)}, u32[]{:S(2)}) %collective-permute-start) | collective-permute-done | bytes 2097184 | tf_op jit(solution)/shard_map/while/body/eval_jaxpr/ppermute | solution.py:19
  193.8 3.9 conditional.3
  199.6 5.9 select_add_fusion.2
  205.6 19.8 %collective-permute-done = bf16[128,8192]{1,0:T(8,128)(2,1)} collective-permute-done((bf16[128,8192]{1,0:T(8,128)(2,1)}, bf16[128,8192]{1,0:T(8,128)(2,1)}, u32[]{:S(2)}, u32[]{:S(2)}) %collective-permute-start) | collective-permute-done | bytes 2097184 | tf_op jit(solution)/shard_map/while/body/eval_jaxpr/ppermute | solution.py:19
  225.4 3.9 conditional.3
  231.2 5.9 select_add_fusion.2
  237.1 19.8 %collective-permute-done = bf16[128,8192]{1,0:T(8,128)(2,1)} collective-permute-done((bf16[128,8192]{1,0:T(8,128)(2,1)}, bf16[128,8192]{1,0:T(8,128)(2,1)}, u32[]{:S(2)}, u32[]{:S(2)}) %collective-permute-start) | collective-permute-done | bytes 2097184 | tf_op jit(solution)/shard_map/while/body/eval_jaxpr/ppermute | solution.py:19
  256.9 3.9 conditional.3
  262.8 5.9 select_add_fusion.2
  268.7 19.8 %collective-permute-done = bf16[128,8192]{1,0:T(8,128)(2,1)} collective-permute-done((bf16[128,8192]{1,0:T(8,128)(2,1)}, bf16[128,8192]{1,0:T(8,128)(2,1)}, u32[]{:S(2)}, u32[]{:S(2)}) %collective-permute-start) | collective-permute-done | bytes 2097184 | tf_op jit(solution)/shard_map/while/body/eval_jaxpr/ppermute | solution.py:19
  288.5 3.9 conditional.3
  294.4 5.9 select_add_fusion.2
  300.3 24.5 %collective-permute-done = bf16[128,8192]{1,0:T(8,128)(2,1)} collective-permute-done((bf16[128,8192]{1,0:T(8,128)(2,1)}, bf16[128,8192]{1,0:T(8,128)(2,1)}, u32[]{:S(2)}, u32[]{:S(2)}) %collective-permute-start) | collective-permute-done | bytes 2097184 | tf_op jit(solution)/shard_map/while/body/eval_jaxpr/ppermute | solution.py:19
  324.8 10.5 conditional.3
  337.3 5.9 select_add_fusion.2
  343.2 19.8 %collective-permute-done = bf16[128,8192]{1,0:T(8,128)(2,1)} collective-permute-done((bf16[128,8192]{1,0:T(8,128)(2,1)}, bf16[128,8192]{1,0:T(8,128)(2,1)}, u32[]{:S(2)}, u32[]{:S(2)}) %collective-permute-start) | collective-permute-done | bytes 2097184 | tf_op jit(solution)/shard_map/while/body/eval_jaxpr/ppermute | solution.py:19
  363.0 3.9 conditional.3
  368.9 5.9 select_add_fusion.2
  374.8 19.8 %collective-permute-done = bf16[128,8192]{1,0:T(8,128)(2,1)} collective-permute-done((bf16[128,8192]{1,0:T(8,128)(2,1)}, bf16[128,8192]{1,0:T(8,128)(2,1)}, u32[]{:S(2)}, u32[]{:S(2)}) %collective-permute-start) | collective-permute-done | bytes 2097184 | tf_op jit(solution)/shard_map/while/body/eval_jaxpr/ppermute | solution.py:19
  394.6 682.9 %reduce-scatter.2.cloned.1.call-done = f32[2,64,128]{2,1,0:T(8,128)} async-done(((f32[2,64,8192]{2,1,0:T(8,128)}), f32[2,64,128]{2,1,0:T(8,128)}) %reduce-scatter.2.cloned.1.call-update) | async-done | bytes 65552 | tf_op jit(solution)/shard_map/reduce_scatter | solution.py:92
  1079.0 112.6 %psum.7 = f32[]{:T(128)} all-reduce(f32[]{:T(128)} %multiply_reduce_fusion), channel_id=1, replica_groups=mesh['pipe'=8,'dp'=64] {'pipe','dp'}, use_global_device_ids=true, to_apply=%region_6.7 | all-reduce | flops 1 | bytes 8 | tf_op jit(solution)/shard_map/psum | solution.py:93
  (51 shorter events, 61.7 us)
Async XLA Ops:
  9.8 114.1 %all-to-all-start = ((bf16[64,2,64,128]{3,2,1,0:T(8,128)(2,1)}), bf16[64,2,64,128]{3,2,1,0:T(8,128)(2,1)S(1)}, u32[]{:S(2)}, u32[]{:S(2)}) async-start(bf16[64,2,64,128]{3,2,1,0:T(8,128)(2,1)} %stack.12), calls=%async_computation | async-start | bytes 4194304 | tf_op jit(solution)/shard_map/all_to_all | solution.py:55
  29.1 37.4 %all-gather.2.cloned.1.call-start = ((), (), s32[]{:S(2)}) async-start(), calls=%async_computation.2 | async-start | bytes 2359296 | tf_op jit(solution)/shard_map/all_gather | solution.py:57
  29.8 1047.8 %reduce-scatter.2.cloned.1.call-start = ((), (), s32[]{:S(2)}) async-start(), calls=%async_computation.3 | async-start | bytes 4259840 | tf_op jit(solution)/shard_map/reduce_scatter | solution.py:92
  125.5 2.3 copy-start
  131.8 30.4 %collective-permute-start = (bf16[128,8192]{1,0:T(8,128)(2,1)}, bf16[128,8192]{1,0:T(8,128)(2,1)}, u32[]{:S(2)}, u32[]{:S(2)}) collective-permute-start(bf16[128,8192]{1,0:T(8,128)(2,1)} %get-tuple-element.300), channel_id=1, source_target_pairs={{64,0},{128,64},{192,128},{256,192},{320,256},{384,320},{448,384},... | collective-permute-start | bytes 6291464 | tf_op jit(solution)/shard_map/while/body/eval_jaxpr/ppermute | solution.py:19
  166.1 27.7 %collective-permute-start = (bf16[128,8192]{1,0:T(8,128)(2,1)}, bf16[128,8192]{1,0:T(8,128)(2,1)}, u32[]{:S(2)}, u32[]{:S(2)}) collective-permute-start(bf16[128,8192]{1,0:T(8,128)(2,1)} %get-tuple-element.300), channel_id=1, source_target_pairs={{64,0},{128,64},{192,128},{256,192},{320,256},{384,320},{448,384},... | collective-permute-start | bytes 6291464 | tf_op jit(solution)/shard_map/while/body/eval_jaxpr/ppermute | solution.py:19
  197.7 27.7 %collective-permute-start = (bf16[128,8192]{1,0:T(8,128)(2,1)}, bf16[128,8192]{1,0:T(8,128)(2,1)}, u32[]{:S(2)}, u32[]{:S(2)}) collective-permute-start(bf16[128,8192]{1,0:T(8,128)(2,1)} %get-tuple-element.300), channel_id=1, source_target_pairs={{64,0},{128,64},{192,128},{256,192},{320,256},{384,320},{448,384},... | collective-permute-start | bytes 6291464 | tf_op jit(solution)/shard_map/while/body/eval_jaxpr/ppermute | solution.py:19
  229.3 27.7 %collective-permute-start = (bf16[128,8192]{1,0:T(8,128)(2,1)}, bf16[128,8192]{1,0:T(8,128)(2,1)}, u32[]{:S(2)}, u32[]{:S(2)}) collective-permute-start(bf16[128,8192]{1,0:T(8,128)(2,1)} %get-tuple-element.300), channel_id=1, source_target_pairs={{64,0},{128,64},{192,128},{256,192},{320,256},{384,320},{448,384},... | collective-permute-start | bytes 6291464 | tf_op jit(solution)/shard_map/while/body/eval_jaxpr/ppermute | solution.py:19
  260.9 27.7 %collective-permute-start = (bf16[128,8192]{1,0:T(8,128)(2,1)}, bf16[128,8192]{1,0:T(8,128)(2,1)}, u32[]{:S(2)}, u32[]{:S(2)}) collective-permute-start(bf16[128,8192]{1,0:T(8,128)(2,1)} %get-tuple-element.300), channel_id=1, source_target_pairs={{64,0},{128,64},{192,128},{256,192},{320,256},{384,320},{448,384},... | collective-permute-start | bytes 6291464 | tf_op jit(solution)/shard_map/while/body/eval_jaxpr/ppermute | solution.py:19
  292.4 32.4 %collective-permute-start = (bf16[128,8192]{1,0:T(8,128)(2,1)}, bf16[128,8192]{1,0:T(8,128)(2,1)}, u32[]{:S(2)}, u32[]{:S(2)}) collective-permute-start(bf16[128,8192]{1,0:T(8,128)(2,1)} %get-tuple-element.300), channel_id=1, source_target_pairs={{64,0},{128,64},{192,128},{256,192},{320,256},{384,320},{448,384},... | collective-permute-start | bytes 6291464 | tf_op jit(solution)/shard_map/while/body/eval_jaxpr/ppermute | solution.py:19
  324.8 2.2 copy-start.2
  327.1 2.2 copy-start.1
  335.4 27.7 %collective-permute-start = (bf16[128,8192]{1,0:T(8,128)(2,1)}, bf16[128,8192]{1,0:T(8,128)(2,1)}, u32[]{:S(2)}, u32[]{:S(2)}) collective-permute-start(bf16[128,8192]{1,0:T(8,128)(2,1)} %get-tuple-element.300), channel_id=1, source_target_pairs={{64,0},{128,64},{192,128},{256,192},{320,256},{384,320},{448,384},... | collective-permute-start | bytes 6291464 | tf_op jit(solution)/shard_map/while/body/eval_jaxpr/ppermute | solution.py:19
  366.9 27.7 %collective-permute-start = (bf16[128,8192]{1,0:T(8,128)(2,1)}, bf16[128,8192]{1,0:T(8,128)(2,1)}, u32[]{:S(2)}, u32[]{:S(2)}) collective-permute-start(bf16[128,8192]{1,0:T(8,128)(2,1)} %get-tuple-element.300), channel_id=1, source_target_pairs={{64,0},{128,64},{192,128},{256,192},{320,256},{384,320},{448,384},... | collective-permute-start | bytes 6291464 | tf_op jit(solution)/shard_map/while/body/eval_jaxpr/ppermute | solution.py:19
  394.6 797.7 %copy-start.3 = (f32[1,2,64,128]{3,2,1,0:T(8,128)S(1)}, f32[1,2,64,128]{3,2,1,0:T(8,128)}, u32[]{:S(2)}) copy-start(f32[1,2,64,128]{3,2,1,0:T(8,128)} %param.16) | copy-start | bytes 196612
  394.6 797.7 %copy-start.4 = (f32[1,2,64,128]{3,2,1,0:T(8,128)S(1)}, f32[1,2,64,128]{3,2,1,0:T(8,128)}, u32[]{:S(2)}) copy-start(f32[1,2,64,128]{3,2,1,0:T(8,128)} %param.15) | copy-start | bytes 196612
  394.6 797.7 %copy-start.5 = (f32[1,2,64,128]{3,2,1,0:T(8,128)S(1)}, f32[1,2,64,128]{3,2,1,0:T(8,128)}, u32[]{:S(2)}) copy-start(f32[1,2,64,128]{3,2,1,0:T(8,128)} %param.14) | copy-start | bytes 196612
Sparse Core Ops, SparseCore 0:
  32.0 34.3 all-gather.1
  394.7 682.7 reduce-scatter.1
